TPU v7x, 512 devices: a whole 4x8x8 slice. The times are simulated.
512 devices in a mesh: dp: 64 (over y_lo, z, core), tensor: 8 (over y_hi, x).
Axes of the slice: x: 4, y: 8 (y_hi: 2, y_lo: 4; y = y_hi * 4 + y_lo), z: 8, core: 2. Of those that a mesh axis runs over, the one named last changes fastest.
Arguments:
- hidden_rows: bfloat16 [4096, 16384], P('dp', 'tensor')
- norm_gain: float32 [16384], P('tensor'), may hold values from 0.5 to 1.5
- key_weight: bfloat16 [512, 16384], P('dp', 'tensor'), may hold values from -0.046875 to 0.046875
- cotangent: bfloat16 [64, 128, 512], P('dp'), may hold values from -16 to 16
- accepted_counts: int32 [64], P('dp'), may hold values from 16 to 64, as said below
- destination: int32 [4096], P('dp'), may hold values from 0 to 63, as said below
Outputs:
- keys: bfloat16 [64, 128, 512], P('dp')
- key_weight_grad: float32 [512, 16384], P('dp', 'tensor')
- gain_grad: float32 [16384], P('tensor')
Inputs may be any that keep to these rules, and one draw needn't show every extreme that they name: `accepted_counts`: rows 0 to the count minus 1 of a replica are accepted; in every draw one replica accepts all its rows and another a quarter of them. `destination`: among one replica's 64 rows no shard is named more than 2 times; in every draw one shard is named exactly 2 times by every replica, all within the first quarter of that replica's rows.
All inputs are finite; a program needn't handle non-finite values.
Results may differ from a plain program's by a relative error of at most 0.0051.
Values may be sent and summed in bfloat16 or wider, within the bound.
A program may use at most 64 MiB of HBM per device.

v0:
```python
import math
import jax
import jax.numpy as jnp
from jax import lax
from jax.sharding import PartitionSpec as P

D = 16384
EPSILON = 1e-05


def slot_layout(dest_rows, count, groups, capacity):
    row_total = dest_rows.shape[0]
    row_order = lax.broadcasted_iota(jnp.int32, (row_total,), 0)
    onehot = (dest_rows[:, None] == lax.broadcasted_iota(jnp.int32, (row_total, groups), 1)).astype(
        jnp.int32
    )
    before = jnp.cumsum(onehot, axis=0) - onehot
    slot_rank = jnp.sum(before * onehot, axis=1)
    accepted = row_order < count
    position = dest_rows * capacity + slot_rank
    filler = jnp.full((groups * capacity,), row_total, jnp.int32)
    filler = filler.at[jnp.where(accepted, position, groups * capacity)].set(row_order, mode="drop")
    return (accepted, position, filler)


def with_blank(source_table):
    return jnp.concatenate(
        [source_table, jnp.zeros((1, source_table.shape[1]), source_table.dtype)], axis=0
    )


def on_device(hidden_rows, norm_gain, key_weight, cotangent, accepted_counts, destination):
    replicas = lax.axis_size("dp")
    own_rows = hidden_rows.shape[0]
    capacity = 2 * own_rows // replicas
    accepted, position, filler = slot_layout(destination, accepted_counts[0], replicas, capacity)
    row_data = lax.all_to_all(
        with_blank(hidden_rows)[filler], "dp", split_axis=0, concat_axis=0, tiled=True
    )
    row_cot = cotangent[0]
    row_float = row_data.astype(jnp.float32)
    squares = lax.psum(jnp.sum(row_float * row_float, axis=1), "tensor")
    normed = (row_float * lax.rsqrt(squares / D + EPSILON)[:, None] * norm_gain[None, :]).astype(
        jnp.bfloat16
    )
    weights_whole = lax.all_gather(key_weight, "dp", axis=0, tiled=True)
    partial_value = lax.dot_general(
        normed, weights_whole, (((1,), (1,)), ((), ())), preferred_element_type=jnp.float32
    )
    backward = jnp.dot(row_cot, weights_whole, preferred_element_type=jnp.float32)
    row_keys = lax.psum(partial_value, "tensor").astype(jnp.bfloat16)
    factor = 1.0 / math.sqrt(own_rows * replicas)
    grad_weight = (
        lax.psum_scatter(
            lax.dot_general(
                row_cot, normed, (((0,), (0,)), ((), ())), preferred_element_type=jnp.float32
            ),
            "dp",
            scatter_dimension=0,
            tiled=True,
        )
        * factor
    )
    gain_term = jnp.sum(backward * normed.astype(jnp.float32), axis=0)
    grad_gain = lax.psum(gain_term, "dp") * factor / norm_gain
    return (row_keys[None], grad_weight, grad_gain)


def solution(mesh):
    return jax.shard_map(
        on_device,
        mesh=mesh,
        in_specs=(
            P("dp", "tensor"),
            P("tensor"),
            P("dp", "tensor"),
            P("dp", None, None),
            P("dp"),
            P("dp"),
        ),
        out_specs=(P("dp", None, None), P("dp", "tensor"), P("tensor")),
        check_vma=False,
    )
```

profile of v0, /device:TPU:6, one launch (start us, length us, event | category | flops | bytes accessed | tf_op | source)
XLA Modules:
  0.0 436.4 jit_solution(2184907873028048254)
XLA Ops:
  7.2 0.7 all-gather.2.cloned.1.call-update
  8.6 0.7 fusion.3
  9.4 1.0 concatenate.3
  10.4 0.8 select_reduce_fusion
  11.3 0.7 compare_select_fusion.1
  11.9 0.8 scatter_custom_fusion
  12.7 0.9 gather_fusion
  13.7 0.3 all_to_all.6
  14.0 32.0 %all_to_all.9 = bf16[64,2,2048]{2,1,0:T(2,128)(2,1)S(1)} all-to-all(bf16[64,2,2048]{2,1,0:T(2,128)(2,1)S(1)} %all_to_all.6), channel_id=1, replica_groups=mesh['dp'=64,'tensor'=8] {'dp'}, dimensions={0} | all-to-all | bytes 1048576 | tf_op jit(solution)/shard_map/all_to_all | solution.py:37
  46.1 0.6 multiply_reduce_fusion
  46.8 23.5 %psum.21 = f32[128]{0:T(128)S(1)} all-reduce(f32[128]{0:T(128)S(1)} %reduce_sum.31), channel_id=1, replica_groups=mesh['dp'=64,'tensor'=8] {'tensor'}, use_global_device_ids=true, to_apply=%region_4.5 | all-reduce | flops 128 | bytes 1024 | tf_op jit(solution)/shard_map/psum | solution.py:42
  70.5 0.6 multiply_convert_fusion
  71.1 0.2 convert_element_type.34
  71.3 2.7 convolution_bitcast_fusion
  74.0 5.4 %copy.12 = f32[512,2048]{1,0:T(8,128)} copy(f32[512,2048]{0,1:T(8,128)} %convolution_bitcast_fusion) | data formatting | bytes 8388608
  79.6 58.5 %all-gather.2.cloned.1.call-done = bf16[512,2048]{1,0:T(8,128)(2,1)} async-done(((bf16[8,2048]{1,0:T(8,128)(2,1)}), bf16[512,2048]{1,0:T(8,128)(2,1)}) %all-gather.2.cloned.1.call-update) | async-done | bytes 2097168 | tf_op jit(solution)/shard_map/all_gather | solution.py:46
  138.1 2.6 fusion.6
  140.7 0.6 fusion
  141.3 137.8 %psum.23 = f32[2048]{0:T(1024)S(1)} all-reduce(f32[2048]{0:T(1024)S(1)} %fusion), channel_id=1, replica_groups=mesh['dp'=64,'tensor'=8] {'dp'}, use_global_device_ids=true, to_apply=%region_8.9 | all-reduce | flops 2048 | bytes 16384 | tf_op jit(solution)/shard_map/psum | solution.py:65
  279.1 0.6 multiply_divide_fusion
  279.7 49.9 %all-reduce.2 = bf16[128,512]{1,0:T(8,128)(2,1)} all-reduce(f32[128,512]{1,0:T(8,128)S(1)} %fusion.6), channel_id=1, replica_groups=mesh['dp'=64,'tensor'=8] {'tensor'}, use_global_device_ids=true, to_apply=%region_5.6 | all-reduce | flops 65536 | bytes 393216 | tf_op jit(solution)/shard_map/psum | solution.py:51
  329.6 97.8 %reduce-scatter.4.cloned.1.call-done = f32[8,2048]{1,0:T(8,128)} async-done(((f32[512,2048]{1,0:T(8,128)}), f32[8,2048]{1,0:T(8,128)}) %reduce-scatter.4.cloned.1.call-update) | async-done | bytes 65552
  427.4 1.2 copy.13
  428.6 0.9 copy.11
  (18 shorter events, 0.7 us)
Async XLA Ops:
  7.2 64.2 %copy-start = (bf16[1,128,512]{2,1,0:T(8,128)(2,1)S(1)}, bf16[1,128,512]{2,1,0:T(8,128)(2,1)}, u32[]{:S(2)}) copy-start(bf16[1,128,512]{2,1,0:T(8,128)(2,1)} %param.9) | copy-start | bytes 393220
  7.2 130.9 %all-gather.2.cloned.1.call-start = ((), (), s32[]{:S(2)}) async-start(), calls=%async_computation.2 | async-start | bytes 2129920 | tf_op jit(solution)/shard_map/all_gather | solution.py:46
  7.9 419.5 %reduce-scatter.4.cloned.1.call-start = ((), (), s32[]{:S(2)}) async-start(), calls=%async_computation.3 | async-start | bytes 4259840
  13.7 56.8 %copy-start.2 = (f32[2048]{0:T(1024)S(1)}, f32[2048]{0:T(1024)}, u32[]{:S(2)}) copy-start(f32[2048]{0:T(1024)} %param.7) | copy-start | bytes 24580
  138.1 2.6 copy-start.1
Sparse Core Ops, SparseCore 0:
  10.2 127.8 all-gather.1
  140.9 286.4 reduce-scatter.3
where the time goes:
time: 437 us; the launch traced here: 436 us
  blocking collectives  243 us (56%)
  waiting for transfers between devices  157 us (36%)
  between operations  14.8 us (3%)
  local copies, waits for them, and re-layouts  11.1 us (3%)
  matrix products  5.84 us (1%)
    psum x1, blocking collectives, on_device(): grad_gain = lax.psum(gain_term, 'dp') * factor / norm_gain  138 us
    unnamed x3, waiting for transfers between devices  98.5 us
    all_gather x1, waiting for transfers between devices, on_device(): weights_whole = lax.all_gather(key_weight, 'dp', axis=0, tiled=True)  58.5 us
    psum x1, blocking collectives, on_device(): row_keys = lax.psum(partial_value, 'tensor').astype(jnp.bfloat16)  49.9 us
    all_to_all x1, blocking collectives, on_device(): lax.all_to_all(with_blank(hidden_rows)[filler], 'dp', split_axis=0, conca...  32 us
    psum x1, blocking collectives, on_device(): squares = lax.psum(jnp.sum(row_float * row_float, axis=1), 'tensor')  23.5 us
  transfers between devices with their start and end apart: 2, of which 2 were waited for; matrix products, arithmetic and copies ran while one was open for 4% of the time, Pallas kernels for 0%

commit v1 on v0

--- a/solution.py
+++ b/solution.py
@@ -43,7 +43,8 @@
     normed = (row_float * lax.rsqrt(squares / D + EPSILON)[:, None] * norm_gain[None, :]).astype(
         jnp.bfloat16
     )
-    weights_whole = lax.all_gather(key_weight, "dp", axis=0, tiled=True)
+    repeated = jnp.stack([key_weight] * lax.axis_size("dp"))
+    weights_whole = jnp.concatenate(lax.all_to_all(repeated, "dp", 0, 0), axis=0)
     partial_value = lax.dot_general(
         normed, weights_whole, (((1,), (1,)), ((), ())), preferred_element_type=jnp.float32
     )

time: 437 us -> 405 us (0.927); the launches traced: 436 us -> 399 us
  waiting for transfers between devices: 157 us -> 104 us
  blocking collectives: 243 us -> 251 us
  starting transfers between devices: 0.08 us -> 6.15 us
    all_gather x1 -> x0, waiting for transfers between devices: 58.5 us -> none  [on_device(): weights_whole = lax.all_gather(key_weight, 'dp', axis=0, tiled=True)]
    all_to_all x0 -> x1, waiting for transfers between devices: none -> 50.1 us  [on_device(): lax.all_to_all(repeated, 'dp', 0, 0)]
    unnamed x3 -> x2, waiting for transfers between devices: 98.5 us -> 53.4 us
    psum x1, blocking collectives: 138 us -> 144 us  [on_device(): grad_gain = lax.psum(gain_term, 'dp') * factor / norm_gain]
    all_to_all x0 -> x1, starting transfers between devices: none -> 6.11 us  [on_device(): lax.all_to_all(repeated, 'dp', 0, 0)]
  transfers between devices with their start and end apart: 2 -> 2, of which waited for: 2 -> 2; matrix products, arithmetic and copies ran while one was open for 4% -> 1% of each run, Pallas kernels for 0% -> 0%
where the time goes in v1:
time: 405 us; the launch traced here: 399 us
  blocking collectives  251 us (62%)
  waiting for transfers between devices  104 us (26%)
  between operations  14.9 us (4%)
  local copies, waits for them, and re-layouts  14.8 us (4%)
  starting transfers between devices  6.15 us (2%)
  other arithmetic  4.26 us (1%)
  matrix products  4.08 us (1%)
    psum x1, blocking collectives, on_device(): grad_gain = lax.psum(gain_term, 'dp') * factor / norm_gain  144 us
    unnamed x2, waiting for transfers between devices  53.4 us
    psum x1, blocking collectives, on_device(): row_keys = lax.psum(partial_value, 'tensor').astype(jnp.bfloat16)  52.1 us
    all_to_all x1, waiting for transfers between devices, on_device(): lax.all_to_all(repeated, 'dp', 0, 0)  50.1 us
    all_to_all x1, blocking collectives, on_device(): lax.all_to_all(with_blank(hidden_rows)[filler], 'dp', split_axis=0, conca...  31.2 us
    psum x1, blocking collectives, on_device(): squares = lax.psum(jnp.sum(row_float * row_float, axis=1), 'tensor')  23.5 us
    unnamed x11, local copies, waits for them, and re-layouts  8.61 us
  transfers between devices with their start and end apart: 2, of which 2 were waited for; matrix products, arithmetic and copies ran while one was open for 1% of the time, Pallas kernels for 0%

profile of v1, /device:TPU:6, one launch (start us, length us, event | category | flops | bytes accessed | tf_op | source)
XLA Modules:
  0.0 398.8 jit_solution(458854444109994631)
XLA Ops:
  7.9 0.7 fusion.8
  8.7 0.8 select_reduce_fusion
  9.6 0.7 compare_select_fusion.1
  10.2 0.8 scatter_custom_fusion
  11.0 1.0 concatenate.3
  12.0 0.9 gather_fusion
  13.3 31.2 %all_to_all.14 = bf16[64,2,2048]{2,1,0:T(2,128)(2,1)S(1)} all-to-all(bf16[64,2,2048]{2,1,0:T(2,128)(2,1)S(1)} %all_to_all.9), channel_id=1, replica_groups=mesh['dp'=64,'tensor'=8] {'dp'}, dimensions={0} | all-to-all | bytes 1048576 | tf_op jit(solution)/shard_map/all_to_all | solution.py:37
  44.6 0.6 multiply_reduce_fusion
  45.3 23.5 %psum.21 = f32[128]{0:T(128)S(1)} all-reduce(f32[128]{0:T(128)S(1)} %reduce_sum.31), channel_id=1, replica_groups=mesh['dp'=64,'tensor'=8] {'tensor'}, use_global_device_ids=true, to_apply=%region_4.5 | all-reduce | flops 128 | bytes 1024 | tf_op jit(solution)/shard_map/psum | solution.py:42
  69.0 0.6 multiply_convert_fusion.1
  69.9 2.7 convolution_bitcast_fusion
  72.6 5.4 %copy.12 = f32[512,2048]{1,0:T(8,128)} copy(f32[512,2048]{0,1:T(8,128)} %convolution_bitcast_fusion) | data formatting | bytes 8388608
  78.0 0.7 copy-done.3
  78.7 1.6 stack.2
  80.3 6.1 %all-to-all-start.1 = ((bf16[64,8,2048]{2,1,0:T(8,128)(2,1)}), bf16[64,8,2048]{2,1,0:T(8,128)(2,1)S(1)}, u32[]{:S(2)}, u32[]{:S(2)}) async-start(bf16[64,8,2048]{2,1,0:T(8,128)(2,1)} %stack.2), calls=%async_computation.1 | async-start | bytes 4194304 | tf_op jit(solution)/shard_map/all_to_all | solution.py:47
  86.4 1.2 reshape.40
  87.6 50.1 %all-to-all-done.1 = bf16[64,8,2048]{2,1,0:T(8,128)(2,1)S(1)} async-done(((bf16[64,8,2048]{2,1,0:T(8,128)(2,1)}), bf16[64,8,2048]{2,1,0:T(8,128)(2,1)S(1)}, u32[]{:S(2)}, u32[]{:S(2)}) %all-to-all-start.1) | async-done | bytes 2097184 | tf_op jit(solution)/shard_map/all_to_all | solution.py:47
  137.7 0.8 fusion.1
  139.5 144.1 %psum.23 = f32[2048]{0:T(1024)S(1)} all-reduce(f32[2048]{0:T(1024)S(1)} %fusion.3), channel_id=1, replica_groups=mesh['dp'=64,'tensor'=8] {'dp'}, use_global_device_ids=true, to_apply=%region_8.9 | all-reduce | flops 2048 | bytes 16384 | tf_op jit(solution)/shard_map/psum | solution.py:66
  283.6 0.6 multiply_divide_fusion
  284.2 52.1 %all-reduce.2 = bf16[128,512]{1,0:T(8,128)(2,1)} all-reduce(f32[128,512]{1,0:T(8,128)S(1)} %fusion.1), channel_id=1, replica_groups=mesh['dp'=64,'tensor'=8] {'tensor'}, use_global_device_ids=true, to_apply=%region_5.6 | all-reduce | flops 65536 | bytes 393216 | tf_op jit(solution)/shard_map/psum | solution.py:52
  336.3 53.4 %reduce-scatter.4.cloned.1.call-done = f32[8,2048]{1,0:T(8,128)} async-done(((f32[512,2048]{1,0:T(8,128)}), f32[8,2048]{1,0:T(8,128)}) %reduce-scatter.4.cloned.1.call-update) | async-done | bytes 65552
  389.8 1.2 copy.13
  391.0 0.9 copy.11
  (20 shorter events, 2.0 us)
Async XLA Ops:
  7.2 62.7 %copy-start = (bf16[1,128,512]{2,1,0:T(8,128)(2,1)S(1)}, bf16[1,128,512]{2,1,0:T(8,128)(2,1)}, u32[]{:S(2)}) copy-start(bf16[1,128,512]{2,1,0:T(8,128)(2,1)} %param.9) | copy-start | bytes 393220
  7.2 382.6 %reduce-scatter.4.cloned.1.call-start = ((), (), s32[]{:S(2)}) async-start(), calls=%async_computation.3 | async-start | bytes 4259840
  13.0 56.1 %copy-start.2 = (f32[2048]{0:T(1024)S(1)}, f32[2048]{0:T(1024)}, u32[]{:S(2)}) copy-start(f32[2048]{0:T(1024)} %param.7) | copy-start | bytes 24580
  77.9 0.8 copy-start.3
  80.3 57.4 %all-to-all-start.1 = ((bf16[64,8,2048]{2,1,0:T(8,128)(2,1)}), bf16[64,8,2048]{2,1,0:T(8,128)(2,1)S(1)}, u32[]{:S(2)}, u32[]{:S(2)}) async-start(bf16[64,8,2048]{2,1,0:T(8,128)(2,1)} %stack.2), calls=%async_computation.1 | async-start | bytes 4194304 | tf_op jit(solution)/shard_map/all_to_all | solution.py:47
  137.7 1.2 copy-start.1
Sparse Core Ops, SparseCore 0:
  78.1 311.6 reduce-scatter.3
